TPU v7x, 128 devices: a whole 4x4x4 slice. The times are simulated.
128 devices in a mesh: grid: 32 (over y, x, z_lo), ipts: 4 (over z_hi, core).
Axes of the slice: x: 4, y: 4, z: 4 (z_hi: 2, z_lo: 2; z = z_hi * 2 + z_lo), core: 2. Of those that a mesh axis runs over, the one named last changes fastest.
Arguments:
- orbitals: bfloat16 [65536, 1024], P(('grid', 'ipts')), may hold values from -1.1953125 to 1.1953125
- targets: bfloat16 [65536, 256], P(('grid', 'ipts')), may hold values from -6 to 6
- points: int32 [4, 4096], P('ipts', 'grid'), may hold values from 0 to 65535, as said below
- potential: bfloat16 [65536, 16384], P('grid', 'ipts'), may hold values from -0.046875 to 0.046875
Outputs:
- exchanged: bfloat16 [65536, 256], P(('grid', 'ipts'))
Inputs may be any that keep to these rules, and one draw needn't show every extreme that they name: Indices are distinct over all groups; each row of points rises strictly, and its entries k * 128 to (k + 1) * 128 - 1 lie in grid rows k * 2048 to (k + 1) * 2048 - 1.
All inputs are finite; a program needn't handle non-finite values.
Results may differ from a plain program's by a relative error of at most 0.0049.
Values may be sent and summed in bfloat16 or wider, within the bound.
No kernel may reach another device: no remote copies, remote signals or barrier semaphores. Data moves between devices by JAX's collectives and lax.ppermute only.
A program may use at most 128 MiB of HBM per device.

v0:
```python
import jax
import jax.numpy as jnp
from jax import lax
from jax.sharding import Mesh
from jax.sharding import PartitionSpec as P

IPTS = ("ipts_0", "ipts_1")
GRID_IPTS = ("grid", "ipts_0", "ipts_1")


def in_order(pieces, dim):
    dims = list(pieces.shape[1:])
    dims[dim] *= pieces.shape[0]
    return jnp.moveaxis(pieces, 0, dim).reshape(dims)


def gather_in_order(value, axes, turns):
    pieces = value
    for k in turns:
        pieces = lax.all_gather(pieces, axes[k])
    done = turns[::-1]
    back = [done.index(k) for k in range(len(axes))]
    pieces = pieces.transpose(*back, *range(len(axes), pieces.ndim))
    return pieces.reshape(-1, *value.shape)


def whole_of(value, axes, turns, dim):
    return in_order(gather_in_order(value, axes, turns), dim)


def split_up(value, dim, length):
    before, after = (value.shape[:dim], value.shape[dim + 1 :])
    return jnp.moveaxis(value.reshape(*before, length, -1, *after), dim, 0)


def sum_at_owner(value, axis, dim):
    pieces = split_up(value, dim, lax.axis_size(axis))
    arrived = lax.all_to_all(pieces, axis, split_axis=0, concat_axis=0, tiled=True)
    return arrived.astype(jnp.float32).sum(axis=0)


def sent_together(arrays, axis, dim, along):
    both = jnp.concatenate(arrays, axis=along)
    whole, at, finished = (lax.all_gather(both, axis, axis=dim, tiled=True), 0, [])
    for a in arrays:
        finished.append(lax.slice_in_dim(whole, at, at + a.shape[along], axis=along))
        at += a.shape[along]
    return tuple(finished)


def summed_on_arrival(value, axis, dim):
    length = lax.axis_size(axis)
    pieces = lax.all_to_all(split_up(value, dim, length), axis, 0, 0, tiled=True)
    return jnp.sum(pieces, axis=0)


def local(orbitals, targets, points, potential):
    groups = lax.axis_size(IPTS)
    own_rows = orbitals.shape[0]
    slab_length = own_rows * groups
    slab_start = lax.axis_index("grid") * slab_length
    whole_slab = lax.all_gather(orbitals, IPTS, axis=0, tiled=True)
    every_group = whole_of(points, IPTS, (0, 1), 0)
    orbital_values = jnp.take(whole_slab, points[0] - slab_start, axis=0)
    offset = every_group - (slab_start + lax.axis_index(IPTS) * own_rows)
    inside = (offset >= 0) & (offset < own_rows)
    clipped = jnp.clip(offset, 0, own_rows - 1)
    picked = jnp.take(targets, clipped, axis=0) * inside[:, :, None].astype(targets.dtype)
    summed = sum_at_owner(picked, IPTS, 0)
    target_values = summed[0].astype(jnp.bfloat16)
    orbital_piece, target_piece = sent_together((orbital_values, target_values), "grid", 0, 1)
    products = lax.dot_general(
        whole_slab, orbital_piece, (((1,), (1,)), ((), ())), preferred_element_type=jnp.float32
    )
    weighted = (potential * products).astype(jnp.bfloat16)
    group_total = jnp.dot(weighted, target_piece, preferred_element_type=jnp.float32)
    summed_rows = summed_on_arrival(group_total, IPTS, 0)
    return (-summed_rows).astype(jnp.bfloat16)


def solution(mesh):
    torus = Mesh(mesh.devices.reshape(mesh.shape["grid"], 2, 2), ("grid", "ipts_0", "ipts_1"))
    placed = (P(GRID_IPTS, None), P(GRID_IPTS, None), P(IPTS, "grid"), P("grid", IPTS))
    return jax.shard_map(
        local, mesh=torus, in_specs=placed, out_specs=P(GRID_IPTS, None), check_vma=False
    )
```

profile of v0, /device:TPU:1, one launch (start us, length us, event | category | flops | bytes accessed | tf_op | source)
XLA Modules:
  0.0 362.0 jit_solution(10757572754428285465)
XLA Ops:
  6.5 0.0 copy-start
  6.5 0.0 all-gather.7.cloned.1.call-start
  6.5 0.7 all-gather.7.cloned.1.call-update
  7.3 6.2 %all-gather.2 = s32[2,1,128]{2,1,0:T(1,128)S(1)} all-gather(s32[1,1,128]{2,1,0:T(1,128)} %bitcast.38), channel_id=2, replica_groups=mesh['grid'=32,'ipts_0'=2,'ipts_1'=2] {'ipts_0'}, dimensions={0}, use_global_device_ids=true | all-gather | bytes 1536 | tf_op jit(solution)/shard_map/all_gather | solution.py:20
  13.5 3.0 all-gather.3
  16.5 0.0 copy-done
  16.5 2.0 gather_fusion.1
  18.5 0.9 select_multiply_fusion
  19.4 5.1 %all-to-all-start = ((bf16[4,1,128,256]{3,2,1,0:T(8,128)(2,1)}), bf16[4,1,128,256]{3,2,1,0:T(8,128)(2,1)S(1)}, u32[]{:S(2)}, u32[]{:S(2)}) async-start(bf16[4,1,128,256]{3,2,1,0:T(8,128)(2,1)} %select_multiply_fusion), calls=%async_computation | async-start | bytes 524288 | tf_op jit(solution)/shard_map/all_to_all | solution.py:38
  24.5 0.0 all-gather.9.cloned.1.call-start
  24.5 0.7 fusion.8
  25.2 0.7 compare_and_fusion.1
  25.8 8.4 %all-to-all-done = bf16[4,1,128,256]{3,2,1,0:T(8,128)(2,1)S(1)} async-done(((bf16[4,1,128,256]{3,2,1,0:T(8,128)(2,1)}), bf16[4,1,128,256]{3,2,1,0:T(8,128)(2,1)S(1)}, u32[]{:S(2)}, u32[]{:S(2)}) %all-to-all-start) | async-done | bytes 262176 | tf_op jit(solution)/shard_map/all_to_all | solution.py:38
  34.3 19.9 %all-gather.7.cloned.1.call-done = bf16[2048,1024]{1,0:T(8,128)(2,1)} async-done(((bf16[512,1024]{1,0:T(8,128)(2,1)}), bf16[2048,1024]{1,0:T(8,128)(2,1)}) %all-gather.7.cloned.1.call-update) | async-done | bytes 4194320 | tf_op jit(solution)/shard_map/all_gather | solution.py:62
  54.2 3.8 %gather_fusion = bf16[128,1024]{1,0:T(8,128)(2,1)S(1)} fusion(bf16[2048,1024]{1,0:T(8,128)(2,1)} %all-gather.7.cloned.1.call-done, s32[1024]{0:T(1024)S(1)} %pad_clamp_fusion.1), kind=kCustom, calls=%fused_computation | custom fusion | bytes 524800 | tf_op jit(solution)/shard_map/jit(_take)/gather | solution.py:64
  57.9 0.1 broadcast_select_fusion
  58.0 0.8 pad_maximum_fusion
  58.8 0.0 all-gather.9.cloned.1.call-update
  58.8 22.6 %copy.8 = bf16[2048,4096]{0,1:T(8,128)(2,1)} copy(bf16[2048,4096]{1,0:T(8,128)(2,1)} %param.7) | data formatting | bytes 33554432 | tf_op args[3]
  81.4 207.0 %all-gather.9.cloned.1.call-done = bf16[4096,1280]{1,0:T(8,128)(2,1)} async-done(((bf16[128,1280]{1,0:T(8,128)(2,1)}), bf16[4096,1280]{1,0:T(8,128)(2,1)}) %all-gather.9.cloned.1.call-update) | async-done | bytes 10485776 | tf_op jit(solution)/shard_map/all_gather | solution.py:44
  288.4 34.1 %fusion.3 = f32[2048,256]{1,0:T(8,128)} fusion(bf16[2048,4096]{0,1:T(8,128)(2,1)} %copy.8, bf16[2048,1024]{1,0:T(8,128)(2,1)} %all-gather.7.cloned.1.call-done, bf16[4096,1280]{1,0:T(8,128)(2,1)} %all-gather.9.cloned.1.call-done), kind=kOutput, calls=%fused_computation.5 | convolution fusion | flops 21500002304 | bytes 33554432 | tf_op jit(solution)/shard_map/dot_general | solution.py:76
  322.5 31.8 %all_to_all.10 = f32[4,512,256]{2,1,0:T(8,128)S(1)} all-to-all(f32[4,512,256]{2,1,0:T(8,128)} %bitcast.32), channel_id=1, replica_groups=mesh['grid'=32,'ipts_0'=2,'ipts_1'=2] {'ipts_0','ipts_1'}, dimensions={0} | all-to-all | bytes 4194304 | tf_op jit(solution)/shard_map/all_to_all | solution.py:53
  354.3 0.2 reduce_sum.22
  354.4 0.7 negate_convert_fusion
  (9 shorter events, 0.1 us)
Async XLA Ops:
  6.5 10.0 %copy-start = (bf16[512,256]{1,0:T(8,128)(2,1)S(1)}, bf16[512,256]{1,0:T(8,128)(2,1)}, u32[]{:S(2)}) copy-start(bf16[512,256]{1,0:T(8,128)(2,1)} %param.5) | copy-start | bytes 786436
  6.5 47.6 %all-gather.7.cloned.1.call-start = ((), (), s32[]{:S(2)}) async-start(), calls=%async_computation.2 | async-start | bytes 5242880 | tf_op jit(solution)/shard_map/all_gather | solution.py:62
  19.4 14.8 %all-to-all-start = ((bf16[4,1,128,256]{3,2,1,0:T(8,128)(2,1)}), bf16[4,1,128,256]{3,2,1,0:T(8,128)(2,1)S(1)}, u32[]{:S(2)}, u32[]{:S(2)}) async-start(bf16[4,1,128,256]{3,2,1,0:T(8,128)(2,1)} %select_multiply_fusion), calls=%async_computation | async-start | bytes 524288 | tf_op jit(solution)/shard_map/all_to_all | solution.py:38
  24.5 263.9 %all-gather.9.cloned.1.call-start = ((), (), s32[]{:S(2)}) async-start(), calls=%async_computation.3 | async-start | bytes 10813440 | tf_op jit(solution)/shard_map/all_gather | solution.py:44
Sparse Core Ops, SparseCore 0:
  9.0 45.0 all-gather.6
  59.0 229.4 all-gather.8
where the time goes:
time: 363 us; the launch traced here: 362 us
  waiting for transfers between devices  236 us (65%)
  blocking collectives  41 us (11%)
  matrix products  34.1 us (9%)
  local copies, waits for them, and re-layouts  28.3 us (8%)
  between operations  13.5 us (4%)
  starting transfers between devices  5.07 us (1%)
  other arithmetic  4.09 us (1%)
    all_gather x1, waiting for transfers between devices, sent_together(): lax.all_gather(both, axis, axis=dim, tiled=True)  207 us
    dot_general x1, matrix products, local(): jnp.dot(weighted, target_piece, preferred_element_type=jnp.float32)  34.1 us
    all_to_all x1, blocking collectives, summed_on_arrival(): lax.all_to_all(split_up(value, dim, length), axis, 0, 0, tiled=True)  31.8 us
    unnamed x3, local copies, waits for them, and re-layouts  22.6 us
    all_gather x1, waiting for transfers between devices, local(): whole_slab = lax.all_gather(orbitals, IPTS, axis=0, tiled=True)  19.9 us
    all_gather x2, blocking collectives, gather_in_order(): pieces = lax.all_gather(pieces, axes[k])  9.21 us
    all_to_all x1, waiting for transfers between devices, sum_at_owner(): lax.all_to_all(pieces, axis, split_axis=0, concat_axis=0, tiled=True)  8.39 us
  transfers between devices with their start and end apart: 3, of which 3 were waited for; matrix products, arithmetic and copies ran while one was open for 7% of the time, Pallas kernels for 0%

commit v1 on v0

--- a/solution.py
+++ b/solution.py
@@ -59,7 +59,9 @@
     own_rows = orbitals.shape[0]
     slab_length = own_rows * groups
     slab_start = lax.axis_index("grid") * slab_length
-    whole_slab = lax.all_gather(orbitals, IPTS, axis=0, tiled=True)
+    whole_slab = jnp.concatenate(
+        lax.all_to_all(jnp.stack([orbitals] * lax.axis_size(IPTS)), IPTS, 0, 0), axis=0
+    )
     every_group = whole_of(points, IPTS, (0, 1), 0)
     orbital_values = jnp.take(whole_slab, points[0] - slab_start, axis=0)
     offset = every_group - (slab_start + lax.axis_index(IPTS) * own_rows)

time: 363 us -> 398 us (1.096)
  waiting for transfers between devices: 236 us -> 257 us
  blocking collectives: 41 us -> 52.5 us
    all_to_all x1, waiting for transfers between devices: 8.39 us -> 48.8 us  [local(): lax.all_to_all(jnp.stack([orbitals] * lax.axis_size(IPTS)), IPTS, 0, 0)]
    all_gather x1 -> x0, waiting for transfers between devices: 19.9 us -> none  [local(): whole_slab = lax.all_gather(orbitals, IPTS, axis=0, tiled=True)]
    all_to_all x0 -> x1, blocking collectives: none -> 11.4 us  [sum_at_owner(): lax.all_to_all(pieces, axis, split_axis=0, concat_axis=0, tiled=True)]
    unnamed x3 -> x5, local copies, waits for them, and re-layouts: 22.6 us -> 22.6 us
  transfers between devices with their start and end apart: 3 -> 2, of which waited for: 3 -> 2; matrix products, arithmetic and copies ran while one was open for 7% -> 6% of each run, Pallas kernels for 0% -> 0%
where the time goes in v1:
time: 398 us; the launch traced here: 397 us
  waiting for transfers between devices  257 us (65%)
  blocking collectives  52.5 us (13%)
  matrix products  34.1 us (9%)
  local copies, waits for them, and re-layouts  32 us (8%)
  between operations  13.5 us (3%)
  starting transfers between devices  5.84 us (1%)
    all_gather x1, waiting for transfers between devices, sent_together(): lax.all_gather(both, axis, axis=dim, tiled=True)  208 us
    all_to_all x1, waiting for transfers between devices, local(): lax.all_to_all(jnp.stack([orbitals] * lax.axis_size(IPTS)), IPTS, 0, 0)  48.8 us
    dot_general x1, matrix products, local(): jnp.dot(weighted, target_piece, preferred_element_type=jnp.float32)  34.1 us
    all_to_all x1, blocking collectives, summed_on_arrival(): lax.all_to_all(split_up(value, dim, length), axis, 0, 0, tiled=True)  31.8 us
    unnamed x5, local copies, waits for them, and re-layouts  22.6 us
    all_to_all x1, blocking collectives, sum_at_owner(): lax.all_to_all(pieces, axis, split_axis=0, concat_axis=0, tiled=True)  11.4 us
    all_gather x2, blocking collectives, gather_in_order(): pieces = lax.all_gather(pieces, axes[k])  9.33 us
  transfers between devices with their start and end apart: 2, of which 2 were waited for; matrix products, arithmetic and copies ran while one was open for 6% of the time, Pallas kernels for 0%

profile of v1, /device:TPU:1, one launch (start us, length us, event | category | flops | bytes accessed | tf_op | source)
XLA Modules:
  0.0 396.6 jit_solution(5509853911635474851)
XLA Ops:
  6.5 0.0 copy-start
  6.5 0.0 copy-start.1
  6.5 6.3 %all-gather.2 = s32[2,1,128]{2,1,0:T(1,128)S(1)} all-gather(s32[1,1,128]{2,1,0:T(1,128)} %bitcast.39), channel_id=2, replica_groups=mesh['grid'=32,'ipts_0'=2,'ipts_1'=2] {'ipts_0'}, dimensions={0}, use_global_device_ids=true | all-gather | bytes 1536 | tf_op jit(solution)/shard_map/all_gather | solution.py:20
  12.9 3.0 all-gather.3
  15.9 0.0 copy-done
  16.0 2.0 gather_fusion.1
  17.9 0.2 select_multiply_fusion
  18.1 11.4 %all_to_all.15 = bf16[4,1,128,256]{3,2,1,0:T(8,128)(2,1)S(1)} all-to-all(bf16[4,1,128,256]{3,2,1,0:T(8,128)(2,1)S(1)} %select_multiply_fusion), channel_id=1, replica_groups=mesh['grid'=32,'ipts_0'=2,'ipts_1'=2] {'ipts_0','ipts_1'}, dimensions={0} | all-to-all | bytes 524288 | tf_op jit(solution)/shard_map/all_to_all | solution.py:38
  29.5 3.7 stack.2
  33.2 5.8 %all-to-all-start = ((bf16[4,512,1024]{2,1,0:T(8,128)(2,1)}), bf16[4,512,1024]{2,1,0:T(8,128)(2,1)}, u32[]{:S(2)}, u32[]{:S(2)}) async-start(bf16[4,512,1024]{2,1,0:T(8,128)(2,1)} %stack.2), calls=%async_computation | async-start | bytes 8388608 | tf_op jit(solution)/shard_map/all_to_all | solution.py:63
  39.0 0.0 all-gather.6.cloned.1.call-start
  39.0 0.0 copy-done.1
  39.1 48.8 %all-to-all-done = bf16[4,512,1024]{2,1,0:T(8,128)(2,1)} async-done(((bf16[4,512,1024]{2,1,0:T(8,128)(2,1)}), bf16[4,512,1024]{2,1,0:T(8,128)(2,1)}, u32[]{:S(2)}, u32[]{:S(2)}) %all-to-all-start) | async-done | bytes 4194336 | tf_op jit(solution)/shard_map/all_to_all | solution.py:63
  88.0 3.8 gather_fusion
  91.7 0.1 broadcast_select_fusion
  91.8 0.8 pad_maximum_fusion
  92.6 0.0 all-gather.6.cloned.1.call-update
  92.6 22.6 %copy.8 = bf16[2048,4096]{0,1:T(8,128)(2,1)} copy(bf16[2048,4096]{1,0:T(8,128)(2,1)} %param.7) | data formatting | bytes 33554432 | tf_op args[3]
  115.2 207.7 %all-gather.6.cloned.1.call-done = bf16[4096,1280]{1,0:T(8,128)(2,1)} async-done(((bf16[128,1280]{1,0:T(8,128)(2,1)}), bf16[4096,1280]{1,0:T(8,128)(2,1)}) %all-gather.6.cloned.1.call-update) | async-done | bytes 10485776 | tf_op jit(solution)/shard_map/all_gather | solution.py:44
  323.0 34.1 %fusion.3 = f32[2048,256]{1,0:T(8,128)} fusion(bf16[2048,4096]{0,1:T(8,128)(2,1)} %copy.8, bf16[2048,1024]{1,0:T(8,128)(2,1)} %bitcast.1, bf16[4096,1280]{1,0:T(8,128)(2,1)} %all-gather.6.cloned.1.call-done), kind=kOutput, calls=%fused_computation.5 | convolution fusion | flops 21500002304 | bytes 33554432 | tf_op jit(solution)/shard_map/dot_general | solution.py:78
  357.0 31.8 %all_to_all.16 = f32[4,512,256]{2,1,0:T(8,128)S(1)} all-to-all(f32[4,512,256]{2,1,0:T(8,128)} %bitcast.33), channel_id=1, replica_groups=mesh['grid'=32,'ipts_0'=2,'ipts_1'=2] {'ipts_0','ipts_1'}, dimensions={0} | all-to-all | bytes 4194304 | tf_op jit(solution)/shard_map/all_to_all | solution.py:53
  388.8 0.2 reduce_sum.22
  389.0 0.7 negate_convert_fusion
  (11 shorter events, 0.1 us)
Async XLA Ops:
  6.5 9.4 %copy-start = (bf16[512,256]{1,0:T(8,128)(2,1)S(1)}, bf16[512,256]{1,0:T(8,128)(2,1)}, u32[]{:S(2)}) copy-start(bf16[512,256]{1,0:T(8,128)(2,1)} %param.5) | copy-start | bytes 786436
  6.5 32.5 %copy-start.1 = (s32[1,128]{1,0:T(1,128)S(1)}, s32[1,128]{1,0:T(1,128)}, u32[]{:S(2)}) copy-start(s32[1,128]{1,0:T(1,128)} %param.6) | copy-start | bytes 1540
  33.2 54.8 %all-to-all-start = ((bf16[4,512,1024]{2,1,0:T(8,128)(2,1)}), bf16[4,512,1024]{2,1,0:T(8,128)(2,1)}, u32[]{:S(2)}, u32[]{:S(2)}) async-start(bf16[4,512,1024]{2,1,0:T(8,128)(2,1)} %stack.2), calls=%async_computation | async-start | bytes 8388608 | tf_op jit(solution)/shard_map/all_to_all | solution.py:63
  39.0 283.9 %all-gather.6.cloned.1.call-start = ((), (), s32[]{:S(2)}) async-start(), calls=%async_computation.3 | async-start | bytes 10813440 | tf_op jit(solution)/shard_map/all_gather | solution.py:44
Sparse Core Ops, SparseCore 0:
  92.7 230.1 all-gather.5
